TPU v7x, 32 devices: a whole 2x2x4 slice. The times are simulated.
32 devices in a mesh: seq: 4 (over y, x), feat: 8 (over z, core).
Axes of the slice: x: 2, y: 2, z: 4, core: 2. Of those that a mesh axis runs over, the one named last changes fastest.
Arguments:
- queries: bfloat16 [3840, 16, 128], P('seq'), may hold values from -32 to 32
- key_vectors: bfloat16 [3840, 16, 128], P('seq'), may hold values from -32 to 32
- values: bfloat16 [3840, 16, 128], P('seq'), may hold values from -6 to 6
- projections: bfloat16 [16, 4096, 128], P(None, 'feat'), may hold values from -4 to 4
Outputs:
- attended: bfloat16 [3840, 16, 128], P('seq', 'feat')
All inputs are finite; a program needn't handle non-finite values.
Results may differ from a plain program's by a relative error of at most 0.012.
Values may be sent and summed in bfloat16 or wider, within the bound.
A program may use at most 128 MiB of HBM per device.

v0:
```python
import jax
import jax.numpy as jnp
from jax import lax
from jax.sharding import PartitionSpec as P

E = 128


def key_exponents(key_vectors, directions, scaling):
    key_dash = (
        jnp.einsum("the,hme->thm", key_vectors, directions, preferred_element_type=jnp.float32)
        * scaling
    )
    key_diag = jnp.sum(jnp.square(key_vectors.astype(jnp.float32)), axis=2) * (
        0.5 * scaling * scaling
    )
    return key_dash - key_diag[:, :, None]


def key_terms(key_expo, key_peak, values):
    key_phi = jnp.exp(key_expo - key_peak[None, :, None]).astype(jnp.bfloat16)
    key_state = jnp.einsum("thm,the->hme", key_phi, values, preferred_element_type=jnp.float32)
    key_mass = jnp.sum(key_phi, axis=0, dtype=jnp.float32)
    return (key_state, key_mass)


def partial_output(query_dash, query_peak, state_half, key_mass):
    query_phi = jnp.exp(query_dash - query_peak[:, :, None]).astype(jnp.bfloat16)
    numerator = jnp.einsum(
        "thm,hme->the", query_phi, state_half, preferred_element_type=jnp.float32
    )
    denominator = jnp.einsum(
        "thm,hm->th", query_phi.astype(jnp.float32), key_mass, precision=lax.Precision.HIGHEST
    )
    return (numerator, denominator)


def shards(queries, key_vectors, values, projections):
    scaling = E ** (-0.25)
    directions = lax.all_to_all(projections, "feat", split_axis=0, concat_axis=1, tiled=True)
    head_share = queries.shape[1] // lax.axis_size("feat")
    start_head = lax.axis_index("feat") * head_share
    own_queries = lax.dynamic_slice_in_dim(queries, start_head, head_share, 1)
    own_keys = lax.dynamic_slice_in_dim(key_vectors, start_head, head_share, 1)
    own_values = lax.dynamic_slice_in_dim(values, start_head, head_share, 1)
    key_expo = key_exponents(own_keys, directions, scaling)
    key_peak = lax.pmax(jnp.max(key_expo, axis=(0, 2)), "seq")
    key_state, key_mass = key_terms(key_expo, key_peak, own_values)
    key_state, key_mass = lax.psum((key_state, key_mass), "seq")
    state_half = key_state.astype(jnp.bfloat16)
    query_dash = (
        jnp.einsum("the,hme->thm", own_queries, directions, preferred_element_type=jnp.float32)
        * scaling
    )
    numerator, denominator = partial_output(
        query_dash, jnp.max(query_dash, axis=2), state_half, key_mass
    )
    return (numerator / denominator[:, :, None]).astype(jnp.bfloat16)


def solution(mesh):
    placed = (
        P("seq", None, None),
        P("seq", None, None),
        P("seq", None, None),
        P(None, "feat", None),
    )
    return jax.shard_map(
        shards, mesh=mesh, in_specs=placed, out_specs=P("seq", "feat", None), check_vma=False
    )
```

profile of v0, /device:TPU:0, one launch (start us, length us, event | category | flops | bytes accessed | tf_op | source)
XLA Modules:
  0.0 290.5 jit_solution(13360563966676854355)
XLA Ops:
  0.0 6.4 %all-to-all-start = ((bf16[16,512,128]{2,1,0:T(8,128)(2,1)}), bf16[16,512,128]{2,1,0:T(8,128)(2,1)S(1)}, u32[]{:S(2)}, u32[]{:S(2)}) async-start(bf16[16,512,128]{2,1,0:T(8,128)(2,1)} %param.7), calls=%async_computation | async-start | bytes 4194304 | tf_op jit(solution)/shard_map/all_to_all | solution.py:40
  6.4 2.1 constant_dynamic-slice_fusion.2
  8.4 2.8 constant_dynamic-slice_fusion.1
  11.2 2.1 constant_dynamic-slice_fusion
  13.3 0.4 multiply_reduce_fusion
  13.7 41.7 %all-to-all-done = bf16[16,512,128]{2,1,0:T(8,128)(2,1)S(1)} async-done(((bf16[16,512,128]{2,1,0:T(8,128)(2,1)}), bf16[16,512,128]{2,1,0:T(8,128)(2,1)S(1)}, u32[]{:S(2)}, u32[]{:S(2)}) %all-to-all-start) | async-done | bytes 2097184 | tf_op jit(solution)/shard_map/all_to_all | solution.py:40
  55.4 0.0 copy-start
  55.4 1.3 copy-done
  56.7 1.7 copy.6
  58.5 12.5 %fusion.2 = (f32[2]{0:T(128)S(1)}, f32[2,960,4096]{2,1,0:T(8,128)}) fusion(f32[960,2]{0,1:T(2,128)S(1)} %broadcast_multiply_fusion, bf16[2,4096,128]{2,1,0:T(8,128)(2,1)S(1)} %bitcast.42, bf16[960,2,128]{2,1,0:T(2,128)(2,1)S(1)} %constant_dynamic-slice_fusion.2), kind=kOutput, calls=%fused_computation.7 | convolution fusion | flops 2036858880 | bytes 34053640 | tf_op jit(solution)/shard_map/the,hme->thm/dot_general | solution.py:11
  71.0 0.0 copy-start.1
  71.0 10.2 %pmax.7 = f32[2]{0:T(128)S(1)} all-reduce(f32[2]{0:T(128)S(1)} %get-tuple-element.9), channel_id=1, replica_groups=mesh['seq'=4,'feat'=8] {'seq'}, use_global_device_ids=true, to_apply=%region_2.0 | all-reduce | flops 2 | bytes 16 | tf_op jit(solution)/shard_map/pmax | solution.py:47
  81.1 14.1 %convert_reduce_fusion = (f32[2,4096]{1,0:T(2,128)S(1)}, bf16[960,2,4096]{2,0,1:T(8,128)(2,1)S(1)}) fusion(f32[2]{0:T(128)S(1)} %pmax.7, f32[960,2]{0,1:T(2,128)S(1)} %broadcast_multiply_fusion, f32[2,960,4096]{2,1,0:T(8,128)} %get-tuple-element.10), kind=kLoop, calls=%fused_computation.5 | loop fusion | flops 47177728 | bytes 47226376 | tf_op jit(solution)/shard_map/reduce_sum | solution.py:23
  95.3 0.0 copy-done.1
  95.3 8.3 %fusion.25 = f32[2,4096,128]{2,1,0:T(8,128)} fusion(bf16[960,2,4096]{2,0,1:T(8,128)(2,1)S(1)} %get-tuple-element.8, bf16[960,2,128]{2,1,0:T(2,128)(2,1)S(1)} %copy-done.1), kind=kOutput, calls=%fused_computation.17 | convolution fusion | flops 2013265920 | bytes 20414464 | tf_op jit(solution)/shard_map/thm,the->hme/dot_general | solution.py:22
  103.6 12.4 %bitcast_reduce_fusion = (f32[960,2]{0,1:T(2,128)S(1)}, f32[2,960,4096]{2,1,0:T(8,128)}) fusion(bf16[2,4096,128]{2,1,0:T(8,128)(2,1)S(1)} %bitcast.43, bf16[960,2,128]{2,1,0:T(2,128)(2,1)S(1)} %constant_dynamic-slice_fusion), kind=kOutput, calls=%fused_computation.1 | convolution fusion | flops 2028992640 | bytes 34053632 | tf_op jit(solution)/shard_map/the,hme->thm/dot_general | solution.py:52
  116.0 142.1 %all-reduce.2 = (bf16[2,4096,128]{2,1,0:T(8,128)(2,1)S(1)}, f32[2,4096]{1,0:T(2,128)S(1)}) all-reduce(f32[2,4096,128]{2,1,0:T(8,128)} %fusion.25, f32[2,4096]{1,0:T(2,128)S(1)} %get-tuple-element.7), channel_id=1, replica_groups=mesh['seq'=4,'feat'=8] {'seq'}, use_global_device_ids=true, to_apply=%region_3.0 | all-reduce | flops 1056768 | bytes 6356992 | tf_op jit(solution)/shard_map/psum | solution.py:49
  258.1 18.6 %fusion.3 = f32[2,1,960]{2,1,0:T(1,128)S(1)} fusion(f32[2,960,4096]{2,1,0:T(8,128)} %get-tuple-element.12, f32[960,2]{0,1:T(2,128)S(1)} %get-tuple-element.11, f32[2,4096,1]{1,0,2:T(2,128)S(1)} %bitcast.45), kind=kOutput, calls=%fused_computation.8 | convolution fusion | flops 117964800 | bytes 31505408 | tf_op jit(solution)/shard_map/thm,hm->th/dot_general | solution.py:32
  276.7 12.5 %fusion.18 = bf16[960,2,128]{2,0,1:T(8,128)(2,1)S(1)} fusion(bf16[2,4096,128]{2,1,0:T(8,128)(2,1)S(1)} %get-tuple-element.5, f32[2,960,4096]{2,1,0:T(8,128)} %get-tuple-element.12, f32[960,2]{0,1:T(2,128)S(1)} %get-tuple-element.11, f32[960,2]{0,1:T(2,128)S(1)} %bitcast.46), kind=kOutput, calls=%fused_computation.13 | convolution fusion | flops 2037350400 | bytes 34061312 | tf_op jit(solution)/shard_map/thm,hme->the/dot_general | solution.py:29
  289.2 1.3 copy.8
  (2 shorter events, 0.0 us)
Async XLA Ops:
  0.0 55.4 %all-to-all-start = ((bf16[16,512,128]{2,1,0:T(8,128)(2,1)}), bf16[16,512,128]{2,1,0:T(8,128)(2,1)S(1)}, u32[]{:S(2)}, u32[]{:S(2)}) async-start(bf16[16,512,128]{2,1,0:T(8,128)(2,1)} %param.7), calls=%async_computation | async-start | bytes 4194304 | tf_op jit(solution)/shard_map/all_to_all | solution.py:40
  55.4 1.4 copy-start
  71.0 24.3 %copy-start.1 = (bf16[960,2,128]{2,1,0:T(2,128)(2,1)S(1)}, bf16[960,2,128]{2,1,0:T(2,128)(2,1)}, u32[]{:S(2)}) copy-start(bf16[960,2,128]{2,1,0:T(2,128)(2,1)} %constant_dynamic-slice_fusion.1) | copy-start | bytes 1474564
where the time goes:
time: 291 us
  blocking collectives  152 us (52%)
  matrix products  64.3 us (22%)
  waiting for transfers between devices  41.7 us (14%)
  other arithmetic  14.5 us (5%)
  local copies, waits for them, and re-layouts  11.3 us (4%)
  starting transfers between devices  6.35 us (2%)
    psum x1, blocking collectives, shards(): key_state, key_mass = lax.psum((key_state, key_mass), 'seq')  142 us
    all_to_all x1, waiting for transfers between devices, shards(): lax.all_to_all(projections, 'feat', split_axis=0, concat_axis=1, tiled=True)  41.7 us
    dot_general x1, matrix products, partial_output(): jnp.einsum('thm,hm->th', query_phi.astype(jnp.float32), key_mass, precisi...  18.6 us
    reduce_sum x1, other arithmetic, key_terms(): key_mass = jnp.sum(key_phi, axis=0, dtype=jnp.float32)  14.1 us
    dot_general x1, matrix products, partial_output(): jnp.einsum('thm,hme->the', query_phi, state_half, preferred_element_type=...  12.5 us
    dot_general x1, matrix products, key_exponents(): jnp.einsum('the,hme->thm', key_vectors, directions, preferred_element_typ...  12.5 us
    dot_general x1, matrix products, shards(): jnp.einsum('the,hme->thm', own_queries, directions, preferred_element_typ...  12.4 us
    pmax x1, blocking collectives, shards(): key_peak = lax.pmax(jnp.max(key_expo, axis=(0, 2)), 'seq')  10.2 us
  transfers between devices with their start and end apart: 1, of which 1 were waited for; matrix products, arithmetic and copies ran while one was open for 3% of the time, Pallas kernels for 0%

commit v1 on v0

--- a/solution.py
+++ b/solution.py
@@ -37,7 +37,12 @@
 
 def shards(queries, key_vectors, values, projections):
     scaling = E ** (-0.25)
-    directions = lax.all_to_all(projections, "feat", split_axis=0, concat_axis=1, tiled=True)
+    directions = jnp.concatenate(
+        lax.all_to_all(
+            jnp.stack(jnp.split(projections, lax.axis_size("feat"), axis=0)), "feat", 0, 0
+        ),
+        axis=1,
+    )
     head_share = queries.shape[1] // lax.axis_size("feat")
     start_head = lax.axis_index("feat") * head_share
     own_queries = lax.dynamic_slice_in_dim(queries, start_head, head_share, 1)

time: 291 us -> 305 us (1.048)
  local copies, waits for them, and re-layouts: 11.3 us -> 24.7 us
    unnamed x4 -> x11, local copies, waits for them, and re-layouts: 1.35 us -> 13.1 us
  transfers between devices with their start and end apart: 1 -> 1, of which waited for: 1 -> 1; matrix products, arithmetic and copies ran while one was open for 3% -> 2% of each run, Pallas kernels for 0% -> 0%
where the time goes in v1:
time: 305 us; the launch traced here: 304 us
  blocking collectives  152 us (50%)
  matrix products  64.3 us (21%)
  waiting for transfers between devices  41.7 us (14%)
  local copies, waits for them, and re-layouts  24.7 us (8%)
  other arithmetic  14.5 us (5%)
  starting transfers between devices  6.35 us (2%)
    psum x1, blocking collectives, shards(): key_state, key_mass = lax.psum((key_state, key_mass), 'seq')  142 us
    all_to_all x1, waiting for transfers between devices, shards(): lax.all_to_all(jnp.stack(jnp.split(projections, lax.axis_size('feat'), ax...  41.7 us
    dot_general x1, matrix products, partial_output(): jnp.einsum('thm,hm->th', query_phi.astype(jnp.float32), key_mass, precisi...  18.6 us
    reduce_sum x1, other arithmetic, key_terms(): key_mass = jnp.sum(key_phi, axis=0, dtype=jnp.float32)  14.2 us
    unnamed x11, local copies, waits for them, and re-layouts  13.1 us
    dot_general x1, matrix products, partial_output(): jnp.einsum('thm,hme->the', query_phi, state_half, preferred_element_type=...  12.5 us
    dot_general x1, matrix products, key_exponents(): jnp.einsum('the,hme->thm', key_vectors, directions, preferred_element_typ...  12.5 us
    dot_general x1, matrix products, shards(): jnp.einsum('the,hme->thm', own_queries, directions, preferred_element_typ...  12.4 us
  transfers between devices with their start and end apart: 1, of which 1 were waited for; matrix products, arithmetic and copies ran while one was open for 2% of the time, Pallas kernels for 0%

profile of v1, /device:TPU:0, one launch (start us, length us, event | category | flops | bytes accessed | tf_op | source)
XLA Modules:
  0.0 303.8 jit_solution(8207512203763111166)
XLA Ops:
  0.0 1.7 bitcast_dynamic-update-slice_fusion.7
  1.7 1.7 bitcast_dynamic-update-slice_fusion.6
  3.3 1.7 bitcast_dynamic-update-slice_fusion.5
  5.0 1.7 bitcast_dynamic-update-slice_fusion.4
  6.7 1.7 bitcast_dynamic-update-slice_fusion.3
  8.4 1.7 bitcast_dynamic-update-slice_fusion.2
  10.0 1.7 bitcast_dynamic-update-slice_fusion.1
  11.7 1.7 bitcast_dynamic-update-slice_fusion
  13.4 6.4 %all-to-all-start = ((bf16[8,2,512,128]{3,2,1,0:T(8,128)(2,1)}), bf16[8,2,512,128]{3,2,1,0:T(8,128)(2,1)S(1)}, u32[]{:S(2)}, u32[]{:S(2)}) async-start(bf16[8,2,512,128]{3,2,1,0:T(8,128)(2,1)} %bitcast_dynamic-update-slice_fusion), calls=%async_computation | async-start | bytes 4194304 | tf_op jit(solution)/shard_map/all_to_all | solution.py:41
  19.7 2.1 constant_dynamic-slice_fusion.2
  21.8 2.8 constant_dynamic-slice_fusion.1
  24.6 2.1 constant_dynamic-slice_fusion
  26.7 0.4 multiply_reduce_fusion
  27.1 41.7 %all-to-all-done = bf16[8,2,512,128]{3,2,1,0:T(8,128)(2,1)S(1)} async-done(((bf16[8,2,512,128]{3,2,1,0:T(8,128)(2,1)}), bf16[8,2,512,128]{3,2,1,0:T(8,128)(2,1)S(1)}, u32[]{:S(2)}, u32[]{:S(2)}) %all-to-all-start) | async-done | bytes 2097184 | tf_op jit(solution)/shard_map/all_to_all | solution.py:41
  68.8 0.0 copy-start
  68.8 1.3 copy-done
  70.1 1.7 copy.5
  71.9 12.5 %fusion.2 = (f32[2]{0:T(128)S(1)}, f32[2,4096,960]{1,2,0:T(8,128)}) fusion(f32[960,2]{0,1:T(2,128)S(1)} %broadcast_multiply_fusion, bf16[2,4096,128]{2,1,0:T(8,128)(2,1)S(1)} %bitcast.56, bf16[960,2,128]{2,1,0:T(2,128)(2,1)S(1)} %constant_dynamic-slice_fusion.2), kind=kOutput, calls=%fused_computation.7 | convolution fusion | flops 2036858880 | bytes 34053640 | tf_op jit(solution)/shard_map/the,hme->thm/dot_general | solution.py:11
  84.3 10.1 %pmax.7 = f32[2]{0:T(128)S(1)} all-reduce(f32[2]{0:T(128)S(1)} %get-tuple-element.9), channel_id=1, replica_groups=mesh['seq'=4,'feat'=8] {'seq'}, use_global_device_ids=true, to_apply=%region_2.0 | all-reduce | flops 2 | bytes 16 | tf_op jit(solution)/shard_map/pmax | solution.py:52
  94.4 0.0 copy-start.1
  94.4 14.2 %convert_reduce_fusion = (f32[2,4096]{1,0:T(2,128)S(1)}, bf16[960,2,4096]{2,0,1:T(8,128)(2,1)S(1)}) fusion(f32[2]{0:T(128)S(1)} %pmax.7, f32[960,2]{0,1:T(2,128)S(1)} %broadcast_multiply_fusion, f32[2,4096,960]{1,2,0:T(8,128)} %get-tuple-element.10), kind=kLoop, calls=%fused_computation.5 | loop fusion | flops 47177728 | bytes 47226376 | tf_op jit(solution)/shard_map/reduce_sum | solution.py:23
  108.6 0.0 copy-done.1
  108.6 8.3 %fusion.25 = f32[2,4096,128]{2,1,0:T(8,128)} fusion(bf16[960,2,4096]{2,0,1:T(8,128)(2,1)S(1)} %get-tuple-element.8, bf16[960,2,128]{2,1,0:T(2,128)(2,1)S(1)} %copy-done.1), kind=kOutput, calls=%fused_computation.17 | convolution fusion | flops 2013265920 | bytes 20414464 | tf_op jit(solution)/shard_map/thm,the->hme/dot_general | solution.py:22
  116.9 12.4 %bitcast_reduce_fusion = (f32[960,2]{0,1:T(2,128)S(1)}, f32[2,4096,960]{1,2,0:T(8,128)}) fusion(bf16[2,4096,128]{2,1,0:T(8,128)(2,1)S(1)} %bitcast.57, bf16[960,2,128]{2,1,0:T(2,128)(2,1)S(1)} %constant_dynamic-slice_fusion), kind=kOutput, calls=%fused_computation.1 | convolution fusion | flops 2028992640 | bytes 34053632 | tf_op jit(solution)/shard_map/the,hme->thm/dot_general | solution.py:57
  129.3 142.1 %all-reduce.2 = (bf16[2,4096,128]{2,1,0:T(8,128)(2,1)S(1)}, f32[2,4096]{1,0:T(2,128)S(1)}) all-reduce(f32[2,4096,128]{2,1,0:T(8,128)} %fusion.25, f32[2,4096]{1,0:T(2,128)S(1)} %get-tuple-element.7), channel_id=1, replica_groups=mesh['seq'=4,'feat'=8] {'seq'}, use_global_device_ids=true, to_apply=%region_3.0 | all-reduce | flops 1056768 | bytes 6356992 | tf_op jit(solution)/shard_map/psum | solution.py:54
  271.4 18.6 %fusion.3 = f32[2,1,960]{2,1,0:T(1,128)S(1)} fusion(f32[2,4096,960]{1,2,0:T(8,128)} %get-tuple-element.12, f32[960,2]{0,1:T(2,128)S(1)} %get-tuple-element.11, f32[2,4096,1]{1,0,2:T(2,128)S(1)} %bitcast.59), kind=kOutput, calls=%fused_computation.8 | convolution fusion | flops 117964800 | bytes 31505408 | tf_op jit(solution)/shard_map/thm,hm->th/dot_general | solution.py:32
  290.0 12.5 %fusion.18 = bf16[960,2,128]{2,0,1:T(8,128)(2,1)S(1)} fusion(bf16[2,4096,128]{2,1,0:T(8,128)(2,1)S(1)} %get-tuple-element.5, f32[2,4096,960]{1,2,0:T(8,128)} %get-tuple-element.12, f32[960,2]{0,1:T(2,128)S(1)} %get-tuple-element.11, f32[960,2]{0,1:T(2,128)S(1)} %bitcast.60), kind=kOutput, calls=%fused_computation.13 | convolution fusion | flops 2037350400 | bytes 34061312 | tf_op jit(solution)/shard_map/thm,hme->the/dot_general | solution.py:29
  302.5 1.3 copy.8
  (2 shorter events, 0.0 us)
Async XLA Ops:
  13.4 55.4 %all-to-all-start = ((bf16[8,2,512,128]{3,2,1,0:T(8,128)(2,1)}), bf16[8,2,512,128]{3,2,1,0:T(8,128)(2,1)S(1)}, u32[]{:S(2)}, u32[]{:S(2)}) async-start(bf16[8,2,512,128]{3,2,1,0:T(8,128)(2,1)} %bitcast_dynamic-update-slice_fusion), calls=%async_computation | async-start | bytes 4194304 | tf_op jit(solution)/shard_map/all_to_all | solution.py:41
  68.8 1.4 copy-start
  94.4 14.2 %copy-start.1 = (bf16[960,2,128]{2,1,0:T(2,128)(2,1)S(1)}, bf16[960,2,128]{2,1,0:T(2,128)(2,1)}, u32[]{:S(2)}) copy-start(bf16[960,2,128]{2,1,0:T(2,128)(2,1)} %constant_dynamic-slice_fusion.1) | copy-start | bytes 1474564
